TPU v7x, 32 devices: a whole 2x2x4 slice. The times are simulated.
32 devices in a mesh: sub: 8 (over z, y), blk: 4 (over x, core).
Axes of the slice: x: 2, y: 2, z: 4, core: 2. Of those that a mesh axis runs over, the one named last changes fastest.
Arguments:
- initial_state: float32 [8, 64, 2048], P('sub', None, 'blk'), may hold values from -6 to 6
- source: bfloat16 [8, 8, 64, 2048], P('sub', None, None, 'blk'), may hold values from -6 to 6
- inverse_diag: float32 [8, 2048], P('sub', 'blk'), may hold values from 0.5 to 0.85
- inverse_off: bfloat16 [8, 2048, 2048], P('sub', None, 'blk'), may hold values from -0.032958984 to 0.032958984
- coupling: float32 [8, 128], P('sub', 'blk'), may hold values from 0.3 to 3
- initial_waves: bfloat16 [8, 128, 512], P('sub', 'blk'), may hold values from -6 to 6
- bucket: int32 [8], P('sub'), may hold values from 0 to 2
- partner: int32 [8, 128], P('sub', 'blk'), may hold values from 0 to 7
- position_of: int32 [8], replicated, may hold values from 0 to 7, each once
Outputs:
- last_state: float32 [8, 64, 2048], P('sub', None, 'blk')
- waveform: float32 [8, 128, 512], P('sub', 'blk')
Inputs may be any that keep to these rules, and one draw needn't show every extreme that they name: A subcircuit of bucket b takes 8 / 2 ** (2 - b) implicit Euler steps. `position_of`: a permutation.
All inputs are finite; a program needn't handle non-finite values.
Results may differ from a plain program's by a relative error of at most 0.0052.
Values may be sent and summed in bfloat16 or wider, within the bound.
A program may use at most 64 MiB of HBM per device.

v0:
```python
import jax
import jax.numpy as jnp
from jax import lax
from jax.sharding import PartitionSpec as P

SWEEPS = 2


def step_count(bucket, refined_points):
    return jnp.where(
        bucket == 0,
        refined_points // 4,
        jnp.where(bucket == 1, refined_points // 2, refined_points),
    ).astype(jnp.int32)


def port_fetch(waves, selector):
    return jnp.einsum(
        "qjr,rjc->qjc",
        selector,
        lax.all_gather(waves, "sub", axis=0, tiled=True),
        preferred_element_type=jnp.float32,
    ).astype(jnp.bfloat16)


def spread_ports(injected, stride):
    padded = jnp.pad(injected[..., None], [(0, 0)] * injected.ndim + [(0, stride - 1)])
    return padded.reshape(injected.shape[:-1] + (injected.shape[-1] * stride,))


def run_together(
    initial_state, source, inverse_diag, inverse_off, coupling, step_total, spacing, incoming
):
    sub_dev, corners, node_block = initial_state.shape
    refined_points = source.shape[1]
    ports_block = coupling.shape[1]
    stride = node_block // ports_block
    spacing_float = spacing.astype(jnp.float32)
    driven = incoming.astype(jnp.float32).reshape(sub_dev, ports_block, refined_points, corners)
    points = jnp.arange(refined_points, dtype=jnp.int32)

    def contract(totals, shard_rows):
        return totals + jnp.einsum(
            "qcn,qnm->qcm", shard_rows, inverse_off, preferred_element_type=jnp.float32
        )

    def advance(time_step_index, carried):
        current, sample_times = carried
        fine_index = (time_step_index + 1) * spacing - 1
        chosen = points[None, :] == fine_index[:, None]
        forcing = jnp.einsum(
            "qf,qfcn->qcn", chosen.astype(jnp.bfloat16), source, preferred_element_type=jnp.float32
        )
        injected = coupling[:, :, None] * jnp.einsum(
            "qf,qjfc->qjc", chosen.astype(jnp.float32), driven, precision=lax.Precision.HIGHEST
        )
        spread = spread_ports(jnp.swapaxes(injected, 1, 2), stride)
        loop_argument = (current + spacing_float[:, None, None] * (forcing + spread)).astype(
            jnp.bfloat16
        )
        loop_argument = lax.optimization_barrier(loop_argument)
        diagonal_term = inverse_diag[:, None, :] * loop_argument.astype(jnp.float32)
        updated = contract(diagonal_term, lax.all_gather(loop_argument, "blk", axis=2, tiled=True))
        active = time_step_index < step_total
        updated = jnp.where(active[:, None, None], updated, current)
        port_values = updated.reshape(sub_dev, corners, ports_block, stride)[:, :, :, 0]
        sample_times = lax.dynamic_update_index_in_dim(
            sample_times, port_values, time_step_index, 1
        )
        return (updated, sample_times)

    sample_times = jnp.zeros((sub_dev, refined_points, corners, ports_block), jnp.float32)
    last_state, sample_times = lax.fori_loop(
        0, refined_points, advance, (initial_state, sample_times)
    )
    kept_values = (points[None, :, None] // spacing[:, None, None] == points[None, None, :]).astype(
        jnp.float32
    )
    waveform = jnp.einsum(
        "qfk,qkcp->qpfc", kept_values, sample_times, precision=lax.Precision.HIGHEST
    )
    return (last_state, waveform.reshape(sub_dev, ports_block, refined_points * corners))


def shards(
    initial_state,
    source,
    inverse_diag,
    inverse_off,
    coupling,
    initial_waves,
    bucket,
    partner,
    position_of,
):
    refined_points = source.shape[1]
    subs_all = position_of.shape[0]
    identities = jnp.arange(subs_all, dtype=jnp.int32)
    located = jnp.sum(
        jnp.where(partner[:, :, None] == identities[None, None, :], position_of[None, None, :], 0),
        axis=2,
    )
    selector = (located[:, :, None] == identities[None, None, :]).astype(jnp.bfloat16)
    step_total = step_count(bucket, refined_points)
    spacing = refined_points // step_total
    waves = initial_waves
    for sweep_index in range(SWEEPS):
        incoming = port_fetch(waves, selector)
        last_state, waveform = run_together(
            initial_state,
            source,
            inverse_diag,
            inverse_off,
            coupling,
            step_total,
            spacing,
            incoming,
        )
        waves = waveform.astype(jnp.bfloat16)
    return (last_state, waveform)


def solution(mesh):
    return jax.shard_map(
        shards,
        mesh=mesh,
        in_specs=(
            P("sub", None, "blk"),
            P("sub", None, None, "blk"),
            P("sub", "blk"),
            P("sub", None, "blk"),
            P("sub", "blk"),
            P("sub", "blk", None),
            P("sub"),
            P("sub", "blk"),
            P(),
        ),
        out_specs=(P("sub", None, "blk"), P("sub", "blk", None)),
        check_vma=False,
    )
```

profile of v0, /device:TPU:0, one launch (start us, length us, event | category | flops | bytes accessed | tf_op | source)
XLA Modules:
  0.0 216.6 jit_solution(17633719554943924317)
XLA Ops:
  3.0 32.8 %all_gather.26 = bf16[8,32,512]{2,1,0:T(8,128)(2,1)S(1)} all-gather(bf16[1,32,512]{2,1,0:T(8,128)(2,1)} %param.20), channel_id=1, replica_groups=mesh['sub'=8,'blk'=4] {'sub'}, dimensions={0}, use_global_device_ids=true | all-gather | bytes 294912 | tf_op jit(solution)/shard_map/all_gather | solution.py:21
  36.2 73.8 %while.36 = (s32[]{:T(128)}, f32[1,64,512]{2,1,0:T(8,128)S(1)}, f32[1,8,64,32]{2,3,1,0:T(8,128)S(1)}, s32[1]{0:T(128)}, f32[1,512]{1,0:T(1,128)}, /*index=5*/f32...) while((s32[]{:T(128)}, f32[1,64,512]{2,1,0:T(8,128)S(1)}, ...), condition=%wide.region_2.3_spmd.clone, body=%wide.region_1.2_spmd.clone.sunk | while | flops 135202832 | bytes 13330811 | solution.py:73
  37.4 1.4 fusion.101
  38.9 5.8 %all_gather.32 = bf16[1,64,2048]{2,1,0:T(8,128)(2,1)S(1)} all-gather(bf16[1,64,512]{2,1,0:T(8,128)(2,1)S(1)} %fusion.102), channel_id=1, replica_groups=mesh['sub'=8,'blk'=4] {'blk'}, dimensions={2}, use_global_device_ids=true | all-gather | bytes 327680 | tf_op jit(solution)/shard_map/while/body/eval_jaxpr/all_gather | solution.py:63
  46.6 1.4 fusion.101
  48.1 5.9 %all_gather.32 = bf16[1,64,2048]{2,1,0:T(8,128)(2,1)S(1)} all-gather(bf16[1,64,512]{2,1,0:T(8,128)(2,1)S(1)} %fusion.102), channel_id=1, replica_groups=mesh['sub'=8,'blk'=4] {'blk'}, dimensions={2}, use_global_device_ids=true | all-gather | bytes 327680 | tf_op jit(solution)/shard_map/while/body/eval_jaxpr/all_gather | solution.py:63
  55.8 1.4 fusion.101
  57.3 5.9 %all_gather.32 = bf16[1,64,2048]{2,1,0:T(8,128)(2,1)S(1)} all-gather(bf16[1,64,512]{2,1,0:T(8,128)(2,1)S(1)} %fusion.102), channel_id=1, replica_groups=mesh['sub'=8,'blk'=4] {'blk'}, dimensions={2}, use_global_device_ids=true | all-gather | bytes 327680 | tf_op jit(solution)/shard_map/while/body/eval_jaxpr/all_gather | solution.py:63
  65.1 1.4 fusion.101
  66.6 5.9 %all_gather.32 = bf16[1,64,2048]{2,1,0:T(8,128)(2,1)S(1)} all-gather(bf16[1,64,512]{2,1,0:T(8,128)(2,1)S(1)} %fusion.102), channel_id=1, replica_groups=mesh['sub'=8,'blk'=4] {'blk'}, dimensions={2}, use_global_device_ids=true | all-gather | bytes 327680 | tf_op jit(solution)/shard_map/while/body/eval_jaxpr/all_gather | solution.py:63
  74.3 1.4 fusion.101
  75.8 5.9 %all_gather.32 = bf16[1,64,2048]{2,1,0:T(8,128)(2,1)S(1)} all-gather(bf16[1,64,512]{2,1,0:T(8,128)(2,1)S(1)} %fusion.102), channel_id=1, replica_groups=mesh['sub'=8,'blk'=4] {'blk'}, dimensions={2}, use_global_device_ids=true | all-gather | bytes 327680 | tf_op jit(solution)/shard_map/while/body/eval_jaxpr/all_gather | solution.py:63
  85.0 5.9 %all_gather.32 = bf16[1,64,2048]{2,1,0:T(8,128)(2,1)S(1)} all-gather(bf16[1,64,512]{2,1,0:T(8,128)(2,1)S(1)} %fusion.102), channel_id=1, replica_groups=mesh['sub'=8,'blk'=4] {'blk'}, dimensions={2}, use_global_device_ids=true | all-gather | bytes 327680 | tf_op jit(solution)/shard_map/while/body/eval_jaxpr/all_gather | solution.py:63
  94.3 5.9 %all_gather.32 = bf16[1,64,2048]{2,1,0:T(8,128)(2,1)S(1)} all-gather(bf16[1,64,512]{2,1,0:T(8,128)(2,1)S(1)} %fusion.102), channel_id=1, replica_groups=mesh['sub'=8,'blk'=4] {'blk'}, dimensions={2}, use_global_device_ids=true | all-gather | bytes 327680 | tf_op jit(solution)/shard_map/while/body/eval_jaxpr/all_gather | solution.py:63
  102.0 1.4 fusion.101
  103.5 5.9 %all_gather.32 = bf16[1,64,2048]{2,1,0:T(8,128)(2,1)S(1)} all-gather(bf16[1,64,512]{2,1,0:T(8,128)(2,1)S(1)} %fusion.102), channel_id=1, replica_groups=mesh['sub'=8,'blk'=4] {'blk'}, dimensions={2}, use_global_device_ids=true | all-gather | bytes 327680 | tf_op jit(solution)/shard_map/while/body/eval_jaxpr/all_gather | solution.py:63
  110.5 30.8 %all_gather.27 = bf16[8,32,512]{2,1,0:T(8,128)(2,1)S(1)} all-gather(bf16[1,32,512]{2,1,0:T(8,128)(2,1)S(1)} %convert_element_type.111), channel_id=1, replica_groups=mesh['sub'=8,'blk'=4] {'sub'}, dimensions={0}, use_global_device_ids=true | all-gather | bytes 294912 | tf_op jit(solution)/shard_map/all_gather | solution.py:21
  141.7 73.8 %while.37 = (s32[]{:T(128)}, f32[1,64,512]{2,1,0:T(8,128)S(1)}, f32[1,8,64,32]{2,3,1,0:T(8,128)S(1)}, s32[1]{0:T(128)}, f32[1,512]{1,0:T(1,128)}, /*index=5*/f32...) while((s32[]{:T(128)}, f32[1,64,512]{2,1,0:T(8,128)S(1)}, ...), condition=%wide.region_4.6_spmd.clone, body=%wide.region_3.5_spmd.clone.sunk | while | flops 135202832 | bytes 13330811 | solution.py:73
  143.0 1.4 fusion.111
  144.5 5.8 %all_gather.33 = bf16[1,64,2048]{2,1,0:T(8,128)(2,1)S(1)} all-gather(bf16[1,64,512]{2,1,0:T(8,128)(2,1)S(1)} %fusion.112), channel_id=1, replica_groups=mesh['sub'=8,'blk'=4] {'blk'}, dimensions={2}, use_global_device_ids=true | all-gather | bytes 327680 | tf_op jit(solution)/shard_map/while/body/eval_jaxpr/all_gather | solution.py:63
  152.1 1.4 fusion.111
  153.6 5.9 %all_gather.33 = bf16[1,64,2048]{2,1,0:T(8,128)(2,1)S(1)} all-gather(bf16[1,64,512]{2,1,0:T(8,128)(2,1)S(1)} %fusion.112), channel_id=1, replica_groups=mesh['sub'=8,'blk'=4] {'blk'}, dimensions={2}, use_global_device_ids=true | all-gather | bytes 327680 | tf_op jit(solution)/shard_map/while/body/eval_jaxpr/all_gather | solution.py:63
  162.9 5.9 %all_gather.33 = bf16[1,64,2048]{2,1,0:T(8,128)(2,1)S(1)} all-gather(bf16[1,64,512]{2,1,0:T(8,128)(2,1)S(1)} %fusion.112), channel_id=1, replica_groups=mesh['sub'=8,'blk'=4] {'blk'}, dimensions={2}, use_global_device_ids=true | all-gather | bytes 327680 | tf_op jit(solution)/shard_map/while/body/eval_jaxpr/all_gather | solution.py:63
  170.6 1.4 fusion.111
  172.1 5.9 %all_gather.33 = bf16[1,64,2048]{2,1,0:T(8,128)(2,1)S(1)} all-gather(bf16[1,64,512]{2,1,0:T(8,128)(2,1)S(1)} %fusion.112), channel_id=1, replica_groups=mesh['sub'=8,'blk'=4] {'blk'}, dimensions={2}, use_global_device_ids=true | all-gather | bytes 327680 | tf_op jit(solution)/shard_map/while/body/eval_jaxpr/all_gather | solution.py:63
  179.8 1.4 fusion.111
  181.3 5.9 %all_gather.33 = bf16[1,64,2048]{2,1,0:T(8,128)(2,1)S(1)} all-gather(bf16[1,64,512]{2,1,0:T(8,128)(2,1)S(1)} %fusion.112), channel_id=1, replica_groups=mesh['sub'=8,'blk'=4] {'blk'}, dimensions={2}, use_global_device_ids=true | all-gather | bytes 327680 | tf_op jit(solution)/shard_map/while/body/eval_jaxpr/all_gather | solution.py:63
  189.1 1.4 fusion.111
  190.6 5.9 %all_gather.33 = bf16[1,64,2048]{2,1,0:T(8,128)(2,1)S(1)} all-gather(bf16[1,64,512]{2,1,0:T(8,128)(2,1)S(1)} %fusion.112), channel_id=1, replica_groups=mesh['sub'=8,'blk'=4] {'blk'}, dimensions={2}, use_global_device_ids=true | all-gather | bytes 327680 | tf_op jit(solution)/shard_map/while/body/eval_jaxpr/all_gather | solution.py:63
  199.8 5.9 %all_gather.33 = bf16[1,64,2048]{2,1,0:T(8,128)(2,1)S(1)} all-gather(bf16[1,64,512]{2,1,0:T(8,128)(2,1)S(1)} %fusion.112), channel_id=1, replica_groups=mesh['sub'=8,'blk'=4] {'blk'}, dimensions={2}, use_global_device_ids=true | all-gather | bytes 327680 | tf_op jit(solution)/shard_map/while/body/eval_jaxpr/all_gather | solution.py:63
  207.5 1.4 fusion.111
  209.0 5.9 %all_gather.33 = bf16[1,64,2048]{2,1,0:T(8,128)(2,1)S(1)} all-gather(bf16[1,64,512]{2,1,0:T(8,128)(2,1)S(1)} %fusion.112), channel_id=1, replica_groups=mesh['sub'=8,'blk'=4] {'blk'}, dimensions={2}, use_global_device_ids=true | all-gather | bytes 327680 | tf_op jit(solution)/shard_map/while/body/eval_jaxpr/all_gather | solution.py:63
  (231 shorter events, 39.2 us)
Async XLA Ops:
  36.2 8.5 %copy-start = (bf16[1,2048,512]{2,1,0:T(8,128)(2,1)S(1)}, bf16[1,2048,512]{2,1,0:T(8,128)(2,1)}, u32[]{:S(2)}) copy-start(bf16[1,2048,512]{2,1,0:T(8,128)(2,1)} %get-tuple-element.845) | copy-start | bytes 6291460 | tf_op jit(solution)/shard_map/while
  36.2 8.5 %copy-start.3 = (f32[1,512]{1,0:T(1,128)S(1)}, f32[1,512]{1,0:T(1,128)}, u32[]{:S(2)}) copy-start(f32[1,512]{1,0:T(1,128)} %get-tuple-element.839) | copy-start | bytes 6148 | tf_op jit(solution)/shard_map/while
  45.4 8.6 %copy-start = (bf16[1,2048,512]{2,1,0:T(8,128)(2,1)S(1)}, bf16[1,2048,512]{2,1,0:T(8,128)(2,1)}, u32[]{:S(2)}) copy-start(bf16[1,2048,512]{2,1,0:T(8,128)(2,1)} %get-tuple-element.845) | copy-start | bytes 6291460 | tf_op jit(solution)/shard_map/while
  45.4 8.6 %copy-start.3 = (f32[1,512]{1,0:T(1,128)S(1)}, f32[1,512]{1,0:T(1,128)}, u32[]{:S(2)}) copy-start(f32[1,512]{1,0:T(1,128)} %get-tuple-element.839) | copy-start | bytes 6148 | tf_op jit(solution)/shard_map/while
  54.6 8.6 %copy-start = (bf16[1,2048,512]{2,1,0:T(8,128)(2,1)S(1)}, bf16[1,2048,512]{2,1,0:T(8,128)(2,1)}, u32[]{:S(2)}) copy-start(bf16[1,2048,512]{2,1,0:T(8,128)(2,1)} %get-tuple-element.845) | copy-start | bytes 6291460 | tf_op jit(solution)/shard_map/while
  54.6 8.5 %copy-start.3 = (f32[1,512]{1,0:T(1,128)S(1)}, f32[1,512]{1,0:T(1,128)}, u32[]{:S(2)}) copy-start(f32[1,512]{1,0:T(1,128)} %get-tuple-element.839) | copy-start | bytes 6148 | tf_op jit(solution)/shard_map/while
  63.9 8.6 %copy-start = (bf16[1,2048,512]{2,1,0:T(8,128)(2,1)S(1)}, bf16[1,2048,512]{2,1,0:T(8,128)(2,1)}, u32[]{:S(2)}) copy-start(bf16[1,2048,512]{2,1,0:T(8,128)(2,1)} %get-tuple-element.845) | copy-start | bytes 6291460 | tf_op jit(solution)/shard_map/while
  63.9 8.6 %copy-start.3 = (f32[1,512]{1,0:T(1,128)S(1)}, f32[1,512]{1,0:T(1,128)}, u32[]{:S(2)}) copy-start(f32[1,512]{1,0:T(1,128)} %get-tuple-element.839) | copy-start | bytes 6148 | tf_op jit(solution)/shard_map/while
  73.1 8.6 %copy-start = (bf16[1,2048,512]{2,1,0:T(8,128)(2,1)S(1)}, bf16[1,2048,512]{2,1,0:T(8,128)(2,1)}, u32[]{:S(2)}) copy-start(bf16[1,2048,512]{2,1,0:T(8,128)(2,1)} %get-tuple-element.845) | copy-start | bytes 6291460 | tf_op jit(solution)/shard_map/while
  73.1 8.6 %copy-start.3 = (f32[1,512]{1,0:T(1,128)S(1)}, f32[1,512]{1,0:T(1,128)}, u32[]{:S(2)}) copy-start(f32[1,512]{1,0:T(1,128)} %get-tuple-element.839) | copy-start | bytes 6148 | tf_op jit(solution)/shard_map/while
  82.3 8.6 %copy-start = (bf16[1,2048,512]{2,1,0:T(8,128)(2,1)S(1)}, bf16[1,2048,512]{2,1,0:T(8,128)(2,1)}, u32[]{:S(2)}) copy-start(bf16[1,2048,512]{2,1,0:T(8,128)(2,1)} %get-tuple-element.845) | copy-start | bytes 6291460 | tf_op jit(solution)/shard_map/while
  82.3 8.5 %copy-start.3 = (f32[1,512]{1,0:T(1,128)S(1)}, f32[1,512]{1,0:T(1,128)}, u32[]{:S(2)}) copy-start(f32[1,512]{1,0:T(1,128)} %get-tuple-element.839) | copy-start | bytes 6148 | tf_op jit(solution)/shard_map/while
  91.6 8.6 %copy-start = (bf16[1,2048,512]{2,1,0:T(8,128)(2,1)S(1)}, bf16[1,2048,512]{2,1,0:T(8,128)(2,1)}, u32[]{:S(2)}) copy-start(bf16[1,2048,512]{2,1,0:T(8,128)(2,1)} %get-tuple-element.845) | copy-start | bytes 6291460 | tf_op jit(solution)/shard_map/while
  91.6 8.5 %copy-start.3 = (f32[1,512]{1,0:T(1,128)S(1)}, f32[1,512]{1,0:T(1,128)}, u32[]{:S(2)}) copy-start(f32[1,512]{1,0:T(1,128)} %get-tuple-element.839) | copy-start | bytes 6148 | tf_op jit(solution)/shard_map/while
  100.8 8.6 %copy-start = (bf16[1,2048,512]{2,1,0:T(8,128)(2,1)S(1)}, bf16[1,2048,512]{2,1,0:T(8,128)(2,1)}, u32[]{:S(2)}) copy-start(bf16[1,2048,512]{2,1,0:T(8,128)(2,1)} %get-tuple-element.845) | copy-start | bytes 6291460 | tf_op jit(solution)/shard_map/while
  100.8 8.5 %copy-start.3 = (f32[1,512]{1,0:T(1,128)S(1)}, f32[1,512]{1,0:T(1,128)}, u32[]{:S(2)}) copy-start(f32[1,512]{1,0:T(1,128)} %get-tuple-element.839) | copy-start | bytes 6148 | tf_op jit(solution)/shard_map/while
  141.8 8.5 %copy-start.1 = (bf16[1,2048,512]{2,1,0:T(8,128)(2,1)S(1)}, bf16[1,2048,512]{2,1,0:T(8,128)(2,1)}, u32[]{:S(2)}) copy-start(bf16[1,2048,512]{2,1,0:T(8,128)(2,1)} %get-tuple-element.887) | copy-start | bytes 6291460 | tf_op jit(solution)/shard_map/while
  141.8 8.5 %copy-start.4 = (f32[1,512]{1,0:T(1,128)S(1)}, f32[1,512]{1,0:T(1,128)}, u32[]{:S(2)}) copy-start(f32[1,512]{1,0:T(1,128)} %get-tuple-element.881) | copy-start | bytes 6148 | tf_op jit(solution)/shard_map/while
  150.9 8.6 %copy-start.1 = (bf16[1,2048,512]{2,1,0:T(8,128)(2,1)S(1)}, bf16[1,2048,512]{2,1,0:T(8,128)(2,1)}, u32[]{:S(2)}) copy-start(bf16[1,2048,512]{2,1,0:T(8,128)(2,1)} %get-tuple-element.887) | copy-start | bytes 6291460 | tf_op jit(solution)/shard_map/while
  150.9 8.6 %copy-start.4 = (f32[1,512]{1,0:T(1,128)S(1)}, f32[1,512]{1,0:T(1,128)}, u32[]{:S(2)}) copy-start(f32[1,512]{1,0:T(1,128)} %get-tuple-element.881) | copy-start | bytes 6148 | tf_op jit(solution)/shard_map/while
  160.1 8.6 %copy-start.1 = (bf16[1,2048,512]{2,1,0:T(8,128)(2,1)S(1)}, bf16[1,2048,512]{2,1,0:T(8,128)(2,1)}, u32[]{:S(2)}) copy-start(bf16[1,2048,512]{2,1,0:T(8,128)(2,1)} %get-tuple-element.887) | copy-start | bytes 6291460 | tf_op jit(solution)/shard_map/while
  160.2 8.6 %copy-start.4 = (f32[1,512]{1,0:T(1,128)S(1)}, f32[1,512]{1,0:T(1,128)}, u32[]{:S(2)}) copy-start(f32[1,512]{1,0:T(1,128)} %get-tuple-element.881) | copy-start | bytes 6148 | tf_op jit(solution)/shard_map/while
  169.4 8.6 %copy-start.1 = (bf16[1,2048,512]{2,1,0:T(8,128)(2,1)S(1)}, bf16[1,2048,512]{2,1,0:T(8,128)(2,1)}, u32[]{:S(2)}) copy-start(bf16[1,2048,512]{2,1,0:T(8,128)(2,1)} %get-tuple-element.887) | copy-start | bytes 6291460 | tf_op jit(solution)/shard_map/while
  169.4 8.6 %copy-start.4 = (f32[1,512]{1,0:T(1,128)S(1)}, f32[1,512]{1,0:T(1,128)}, u32[]{:S(2)}) copy-start(f32[1,512]{1,0:T(1,128)} %get-tuple-element.881) | copy-start | bytes 6148 | tf_op jit(solution)/shard_map/while
  178.6 8.6 %copy-start.1 = (bf16[1,2048,512]{2,1,0:T(8,128)(2,1)S(1)}, bf16[1,2048,512]{2,1,0:T(8,128)(2,1)}, u32[]{:S(2)}) copy-start(bf16[1,2048,512]{2,1,0:T(8,128)(2,1)} %get-tuple-element.887) | copy-start | bytes 6291460 | tf_op jit(solution)/shard_map/while
  178.6 8.6 %copy-start.4 = (f32[1,512]{1,0:T(1,128)S(1)}, f32[1,512]{1,0:T(1,128)}, u32[]{:S(2)}) copy-start(f32[1,512]{1,0:T(1,128)} %get-tuple-element.881) | copy-start | bytes 6148 | tf_op jit(solution)/shard_map/while
  187.9 8.6 %copy-start.1 = (bf16[1,2048,512]{2,1,0:T(8,128)(2,1)S(1)}, bf16[1,2048,512]{2,1,0:T(8,128)(2,1)}, u32[]{:S(2)}) copy-start(bf16[1,2048,512]{2,1,0:T(8,128)(2,1)} %get-tuple-element.887) | copy-start | bytes 6291460 | tf_op jit(solution)/shard_map/while
  187.9 8.6 %copy-start.4 = (f32[1,512]{1,0:T(1,128)S(1)}, f32[1,512]{1,0:T(1,128)}, u32[]{:S(2)}) copy-start(f32[1,512]{1,0:T(1,128)} %get-tuple-element.881) | copy-start | bytes 6148 | tf_op jit(solution)/shard_map/while
  197.1 8.6 %copy-start.1 = (bf16[1,2048,512]{2,1,0:T(8,128)(2,1)S(1)}, bf16[1,2048,512]{2,1,0:T(8,128)(2,1)}, u32[]{:S(2)}) copy-start(bf16[1,2048,512]{2,1,0:T(8,128)(2,1)} %get-tuple-element.887) | copy-start | bytes 6291460 | tf_op jit(solution)/shard_map/while
  197.1 8.6 %copy-start.4 = (f32[1,512]{1,0:T(1,128)S(1)}, f32[1,512]{1,0:T(1,128)}, u32[]{:S(2)}) copy-start(f32[1,512]{1,0:T(1,128)} %get-tuple-element.881) | copy-start | bytes 6148 | tf_op jit(solution)/shard_map/while
  206.3 8.6 %copy-start.1 = (bf16[1,2048,512]{2,1,0:T(8,128)(2,1)S(1)}, bf16[1,2048,512]{2,1,0:T(8,128)(2,1)}, u32[]{:S(2)}) copy-start(bf16[1,2048,512]{2,1,0:T(8,128)(2,1)} %get-tuple-element.887) | copy-start | bytes 6291460 | tf_op jit(solution)/shard_map/while
  206.3 8.6 %copy-start.4 = (f32[1,512]{1,0:T(1,128)S(1)}, f32[1,512]{1,0:T(1,128)}, u32[]{:S(2)}) copy-start(f32[1,512]{1,0:T(1,128)} %get-tuple-element.881) | copy-start | bytes 6148 | tf_op jit(solution)/shard_map/while
  (1 other events, 1.0 us)
where the time goes:
time: 217 us
  blocking collectives  157 us (72%)
  matrix products  35 us (16%)
  other arithmetic  15 us (7%)
  local copies, waits for them, and re-layouts  6.51 us (3%)
    all_gather x16, blocking collectives, advance(): lax.all_gather(loop_argument, 'blk', axis=2, tiled=True)  93.5 us
    all_gather x2, blocking collectives, port_fetch(): lax.all_gather(waves, 'sub', axis=0, tiled=True)  63.5 us
    dot_general x16, matrix products, advance(): jnp.einsum('qf,qfcn->qcn', chosen.astype(jnp.bfloat16), source, preferred...  23.2 us
    mul x16, other arithmetic, advance(): coupling[:, :, None]  13.5 us
    dot_general x16, matrix products, contract(): jnp.einsum('qcn,qnm->qcm', shard_rows, inverse_off, preferred_element_typ...  7.7 us

commit v1 on v0

v1 whole, which is shorter than its diff:
```python
import functools

import jax
import jax.numpy as jnp
from jax import lax
from jax.experimental import pallas as pl
from jax.experimental.pallas import tpu as pltpu
from jax.sharding import PartitionSpec as P

MESH = pl.DeviceIdType.MESH
BF16 = jnp.bfloat16
F32 = jnp.float32


def mm(a, b):
    return jnp.dot(a, b, preferred_element_type=F32)


def mm_nt(a, b):
    return lax.dot_general(a, b, (((1,), (1,)), ((), ())), preferred_element_type=F32)


def split(v):
    hi = v.astype(BF16)
    return hi, (v - hi.astype(F32)).astype(BF16)


def kernel(
    ns, nb,
    x0, src, dia, moff, cpl, w0, bkt, par, pos,
    last, wav,
    mats, buf, oper, z, hs, p_hi, p_lo, t_hi, t_lo, zp, inc8, rb, samp, wall, iall, call, lhs,
    m_sem, x_send, x_recv, w_send, w_recv, i_send, i_recv,
):
    me_s, me = lax.axis_index("sub"), lax.axis_index("blk")
    steps, rows, width = src.shape[1:]
    ports = cpl.shape[1]
    stride = width // ports
    all_ports = ports * nb
    halves = all_ports // rows
    near = me + 1 - 2 * lax.rem(me, 2)
    across = lax.rem(me + 2, nb)
    roles = (me, near, across, nb - 1 - me)

    loads = [
        pltpu.make_async_copy(
            moff.at[0, pl.ds(pl.multiple_of(b * width, width), width)], mats.at[r], m_sem.at[r]
        )
        for r, b in enumerate(roles)
    ]
    for load in loads:
        load.start()

    barrier = pltpu.get_barrier_semaphore()

    @pl.loop(1, ns)
    def _(d):
        pl.semaphore_signal(
            barrier, inc=1, device_id={"sub": lax.rem(me_s + d, ns)}, device_id_type=MESH
        )

    for peer in roles[1:]:
        pl.semaphore_signal(barrier, inc=1, device_id={"blk": peer}, device_id_type=MESH)

    bucket = bkt[0]
    count = jnp.where(bucket == 0, steps // 4, jnp.where(bucket == 1, steps // 2, steps))
    spacing = jnp.where(bucket == 0, 4, jnp.where(bucket == 1, 2, 1))
    spacing_f = spacing.astype(F32)

    def fine(j):
        return jnp.minimum((j + 1) * spacing - 1, steps - 1)

    def held(g):
        return jnp.where(bucket == 0, g // 4, jnp.where(bucket == 1, g // 2, g))

    def exchange(g, k, role):
        start, end, peer = {1: (0, 1, near), 2: (0, 2, across), 3: (2, 3, near)}[role]
        parity = lax.rem(k, 2)
        return pltpu.make_async_remote_copy(
            src_ref=buf.at[g, k, start],
            dst_ref=buf.at[g, k, end],
            send_sem=x_send.at[g, parity, role - 1],
            recv_sem=x_recv.at[g, parity, role - 1],
            device_id={"blk": peer},
            device_id_type=MESH,
        )

    def post(g, k, value):
        buf[g, k, 0] = value.astype(BF16)
        exchange(g, k, 2).start()
        exchange(g, k, 1).start()

    def finish(g, k):
        exchange(g, k, 2).wait_recv()
        exchange(g, k, 3).start()
        total = diagonal * oper[g] + mm(buf[g, k, 0], mats[0])
        exchange(g, k, 1).wait_recv()
        total += mm(buf[g, k, 1], mats[1])
        total += mm(buf[g, k, 2], mats[2])
        exchange(g, k, 3).wait_recv()
        total += mm(buf[g, k, 3], mats[3])
        for role in (1, 2, 3):
            exchange(g, k, role).wait_send()
        return total

    def wave_copy(t, d):
        return pltpu.make_async_remote_copy(
            src_ref=wall.at[t, me_s],
            dst_ref=wall.at[t, me_s],
            send_sem=w_send.at[t, d],
            recv_sem=w_recv.at[t, me_s],
            device_id={"sub": lax.rem(me_s + d, ns)},
            device_id_type=MESH,
        )

    def send_waves(t):
        @pl.loop(1, ns)
        def _(d):
            wave_copy(t, d).start()

    def wait_waves(t):
        @pl.loop(1, ns)
        def _(d):
            origin = lax.rem(me_s + d, ns)
            pltpu.make_async_remote_copy(
                src_ref=wall.at[t, origin],
                dst_ref=wall.at[t, origin],
                send_sem=w_send.at[t, d],
                recv_sem=w_recv.at[t, origin],
                device_id={"sub": origin},
                device_id_type=MESH,
            ).wait_recv()

    def block_copy(ref, t, r, owner):
        return pltpu.make_async_remote_copy(
            src_ref=ref.at[owner],
            dst_ref=ref.at[owner],
            send_sem=i_send.at[t, r],
            recv_sem=i_recv.at[t, owner],
            device_id={"blk": roles[r]},
            device_id_type=MESH,
        )

    def share(ref, t):
        for r in (2, 3, 1):
            block_copy(ref, t, r, me).start()

    def wait_share(ref, t):
        for r in (1, 2, 3):
            block_copy(ref, t, r, roles[r]).wait_recv()

    square = (
        lax.broadcasted_iota(jnp.int32, (ports, ports), 0)
        == lax.broadcasted_iota(jnp.int32, (ports, ports), 1)
    )

    def column(row):
        spread = jnp.broadcast_to(row, (ports, ports))
        return jnp.sum(jnp.where(square, spread, jnp.zeros_like(spread)), axis=1, keepdims=True)

    def select(t):
        owner = column(par[...].astype(F32))

        def place(i, found):
            return jnp.where(owner == i.astype(F32), pos[i].astype(F32), found)

        located = lax.fori_loop(0, ns, place, jnp.zeros((ports, 1), F32))

        def pick(q, chosen):
            return jnp.where(located == q.astype(F32), wall[t, q].astype(F32), chosen)

        chosen = lax.fori_loop(0, ns, pick, jnp.zeros(w0.shape[1:], F32))
        iall[t, me] = chosen.astype(BF16)

    def inputs(t):
        for b in range(nb):
            value = iall[t, b]
            for f in range(steps):
                inc8[f, b * ports : (b + 1) * ports, :] = value[:, f * rows : (f + 1) * rows]
        for j in range(steps):
            factor = jnp.where(j < count, spacing_f, 0.0)
            rb[j] = (inc8[fine(j)].astype(F32) * factor).astype(BF16)

    def respond():
        drive = rb[...].reshape(steps * all_ports, rows)
        value = mm(t_hi[...], drive) + mm(t_lo[...], drive)
        samp[...] = zp[...] + value.reshape(steps, ports, rows)

    diagonal = dia[...]
    pick_ports = (
        lax.broadcasted_iota(jnp.int32, (ports, width), 1)
        == stride * lax.broadcasted_iota(jnp.int32, (ports, width), 0)
    ).astype(F32).astype(BF16)

    z[...] = x0[0]
    wall[0, me_s] = w0[0]
    call[me] = jnp.broadcast_to(column(cpl[...]), call.shape[1:])
    first = x0[0] + spacing_f * src[0, fine(0)].astype(F32)
    oper[0] = first

    pl.semaphore_wait(barrier, ns - 1 + nb - 1)
    post(0, 0, first)
    share(call, 2)
    send_waves(0)
    t_hi[...] = jnp.zeros_like(t_hi)
    t_lo[...] = jnp.zeros_like(t_lo)
    for load in loads:
        load.wait()

    def keep(h, k, value):
        scale = call[...].reshape(all_ports, call.shape[2])[h * rows : (h + 1) * rows, :1]
        hi, lo = split(scale * value)
        hs[k, h * rows : (h + 1) * rows, :] = hi
        p_hi[k, :, h * rows : (h + 1) * rows] = mm_nt(pick_ports, hi).astype(BF16)
        p_lo[k, :, h * rows : (h + 1) * rows] = mm_nt(pick_ports, lo).astype(BF16)

    for h in range(halves):
        node = stride * (lax.broadcasted_iota(jnp.int32, (rows, width), 0) + h * rows)
        lane = lax.broadcasted_iota(jnp.int32, (rows, width), 1)
        total = diagonal * (lane + me * width == node).astype(F32)
        for r, b in enumerate(roles):
            total += mm((lane + b * width == node).astype(F32).astype(BF16), mats[r])
        oper[1 + h] = total
        post(1 + h, 1, total)
    wait_share(call, 2)
    for h in range(halves):
        keep(h, 0, oper[1 + h])

    @pl.loop(0, steps)
    def _(i):
        total = jnp.where(i < count, finish(0, i), z[...])
        z[...] = total

        @pl.when(i < steps - 1)
        def _():
            operand = total + spacing_f * src[0, fine(i + 1)].astype(F32)
            oper[0] = operand
            post(0, i + 1, operand)

        hi, lo = split(total)
        zp[i] = mm_nt(pick_ports, hi) + mm_nt(pick_ports, lo)

        @pl.when(i >= 1)
        def _():
            for h in range(halves):
                value = finish(1 + h, i)
                oper[1 + h] = value

                @pl.when(i < steps - 1)
                def _():
                    post(1 + h, i + 1, value)

                keep(h, i, value)

        @pl.when(i == steps // 2 - 1)
        def _():
            wait_waves(0)
            select(0)
            share(iall.at[0], 0)

        @pl.when(i == steps // 2 + 1)
        def _():
            wait_share(iall.at[0], 0)
            inputs(0)

    for k in range(steps):
        for j in range(k + 1):
            there = (
                slice(k * ports, (k + 1) * ports),
                slice(j * all_ports, (j + 1) * all_ports),
            )
            t_hi[there] = p_hi[k - j]
            t_lo[there] = p_lo[k - j]
    respond()
    for g in range(steps):
        wall[1, me_s, :, g * rows : (g + 1) * rows] = samp[held(g)].astype(BF16)
    send_waves(1)
    wait_waves(1)
    select(1)
    share(iall.at[1], 1)
    wait_share(iall.at[1], 1)
    inputs(1)
    respond()
    for g in range(steps):
        wav[0, :, g * rows : (g + 1) * rows] = samp[held(g)]
    unit = (
        lax.broadcasted_iota(jnp.int32, (rows, rows), 0)
        == lax.broadcasted_iota(jnp.int32, (rows, rows), 1)
    ).astype(F32).astype(BF16)
    for m in range(1, steps + 1):
        turned = mm_nt(unit, rb[jnp.maximum(count - m, 0)])
        lhs[:, (m - 1) * all_ports : m * all_ports] = jnp.where(m <= count, turned, 0.0).astype(BF16)
    last[0] = z[...] + mm(lhs[...], hs[...].reshape(steps * all_ports, width))

    for t in range(2):

        @pl.loop(1, ns)
        def _(d):
            wave_copy(t, d).wait_send()

        for r in (1, 2, 3):
            block_copy(iall.at[t], t, r, me).wait_send()
    for r in (1, 2, 3):
        block_copy(call, 2, r, me).wait_send()


def shards(ns, nb, initial_state, source, inverse_diag, inverse_off, coupling, initial_waves,
           bucket, partner, position_of):
    _, steps, rows, width = source.shape
    ports = coupling.shape[1]
    all_ports = ports * nb
    groups = 1 + all_ports // rows
    vmem = pl.BlockSpec(memory_space=pltpu.VMEM)
    smem = pl.BlockSpec(memory_space=pltpu.SMEM)
    dma = pltpu.SemaphoreType.DMA
    return pl.pallas_call(
        functools.partial(kernel, ns, nb),
        out_shape=(
            jax.ShapeDtypeStruct(initial_state.shape, F32),
            jax.ShapeDtypeStruct(initial_waves.shape, F32),
        ),
        in_specs=[vmem, vmem, vmem, pl.BlockSpec(memory_space=pl.ANY), vmem, vmem, smem, vmem, smem],
        out_specs=(vmem, vmem),
        scratch_shapes=[
            pltpu.VMEM((nb, width, width), BF16),
            pltpu.VMEM((groups, steps, nb, rows, width), BF16),
            pltpu.VMEM((groups, rows, width), F32),
            pltpu.VMEM((rows, width), F32),
            pltpu.VMEM((steps, all_ports, width), BF16),
            pltpu.VMEM((steps, ports, all_ports), BF16),
            pltpu.VMEM((steps, ports, all_ports), BF16),
            pltpu.VMEM((steps * ports, steps * all_ports), BF16),
            pltpu.VMEM((steps * ports, steps * all_ports), BF16),
            pltpu.VMEM((steps, ports, rows), F32),
            pltpu.VMEM((steps, all_ports, rows), BF16),
            pltpu.VMEM((steps, all_ports, rows), BF16),
            pltpu.VMEM((steps, ports, rows), F32),
            pltpu.VMEM((2, ns) + initial_waves.shape[1:], BF16),
            pltpu.VMEM((2, nb) + initial_waves.shape[1:], BF16),
            pltpu.VMEM((nb, ports, 128), F32),
            pltpu.VMEM((rows, steps * all_ports), BF16),
            dma((nb,)),
            dma((groups, 2, 3)),
            dma((groups, 2, 3)),
            dma((2, ns)),
            dma((2, ns)),
            dma((3, nb)),
            dma((3, nb)),
        ],
        compiler_params=pltpu.CompilerParams(
            collective_id=0, has_side_effects=True, vmem_limit_bytes=48 * 1024 * 1024
        ),
    )(initial_state, source, inverse_diag, inverse_off, coupling, initial_waves, bucket, partner,
      position_of)


def solution(mesh):
    return jax.shard_map(
        functools.partial(shards, mesh.shape["sub"], mesh.shape["blk"]),
        mesh=mesh,
        in_specs=(
            P("sub", None, "blk"),
            P("sub", None, None, "blk"),
            P("sub", "blk"),
            P("sub", None, "blk"),
            P("sub", "blk"),
            P("sub", "blk", None),
            P("sub"),
            P("sub", "blk"),
            P(),
        ),
        out_specs=(P("sub", None, "blk"), P("sub", "blk", None)),
        check_vma=False,
    )
```

time: 217 us -> 72.1 us (0.33)
  blocking collectives: 157 us -> 0 us
  Pallas kernels: 0 us -> 62.3 us
  matrix products: 35 us -> 0 us
  other arithmetic: 15 us -> 0 us
    all_gather x18 -> x0, blocking collectives: 157 us -> none  [the longest x16 93.5 us: advance(): lax.all_gather(loop_argument, 'blk', axis=2, tiled=True)]
    pallas_call x0 -> x1, Pallas kernels: none -> 62.3 us  [shards(): pl.pallas_call(functools.partial(kernel, ns, nb), out_shape=(jax.ShapeDty...]
    dot_general x52 -> x0, matrix products: 35 us -> none  [the longest x16 23.2 us: advance(): jnp.einsum('qf,qfcn->qcn', chosen.astype(jnp.bfloat16), source, preferred...]
    mul x16 -> x0, other arithmetic: 13.5 us -> none  [advance(): coupling[:, :, None]]
    unnamed x4 -> x18, local copies, waits for them, and re-layouts: 0.92 us -> 8.22 us
    reshape x19 -> x0, local copies, waits for them, and re-layouts: 2.68 us -> none  [the longest x16 1.79 us: spread_ports(): return padded.reshape(injected.shape[:-1] + (injected.shape[-1] * stride,))]
where the time goes in v1:
time: 72.1 us; the launch traced here: 71.8 us
  Pallas kernels  62.3 us (86%)
  local copies, waits for them, and re-layouts  8.22 us (11%)
  between operations  1.3 us (2%)
    pallas_call x1, Pallas kernels, shards(): pl.pallas_call(functools.partial(kernel, ns, nb), out_shape=(jax.ShapeDty...  62.3 us
    unnamed x18, local copies, waits for them, and re-layouts  8.22 us

profile of v1, /device:TPU:0, one launch (start us, length us, event | category | flops | bytes accessed | tf_op | source)
XLA Modules:
  0.0 71.8 jit_solution(15644554204611802812)
XLA Ops:
  1.3 0.0 copy-start
  1.3 1.6 %copy-done = bf16[1,2048,512]{2,1,0:T(8,128)(2,1)S(1)} copy-done((bf16[1,2048,512]{2,1,0:T(8,128)(2,1)S(1)}, bf16[1,2048,512]{2,1,0:T(8,128)(2,1)}, u32[]{:S(2)}) %copy-start) | copy-done | bytes 2097176
  2.9 0.0 copy-start.1
  2.9 1.0 %copy-done.1 = bf16[1,8,64,512]{3,2,1,0:T(8,128)(2,1)S(1)} copy-done((bf16[1,8,64,512]{3,2,1,0:T(8,128)(2,1)S(1)}, bf16[1,8,64,512]{3,2,1,0:T(8,128)(2,1)}, u32[]{:S(2)}) %copy-start.1) | copy-done | bytes 524312
  3.9 0.0 copy-start.2
  3.9 0.9 %copy-done.2 = f32[1,64,512]{2,1,0:T(8,128)S(1)} copy-done((f32[1,64,512]{2,1,0:T(8,128)S(1)}, f32[1,64,512]{2,1,0:T(8,128)}, u32[]{:S(2)}) %copy-start.2) | copy-done | bytes 131096
  4.8 0.0 copy-start.3
  4.8 0.8 %copy-done.3 = bf16[1,32,512]{2,1,0:T(8,128)(2,1)S(1)} copy-done((bf16[1,32,512]{2,1,0:T(8,128)(2,1)S(1)}, bf16[1,32,512]{2,1,0:T(8,128)(2,1)}, u32[]{:S(2)}) %copy-start.3) | copy-done | bytes 32792
  5.6 0.0 copy-start.4
  5.6 0.7 copy-done.4
  6.3 0.0 copy-start.5
  6.3 0.7 copy-done.5
  6.9 0.0 copy-start.6
  6.9 0.7 copy-done.6
  7.6 0.0 copy-start.7
  7.6 0.7 copy-done.7
  8.2 62.3 %shard_map.104 = (f32[1,64,512]{2,1,0:T(8,128)S(1)}, f32[1,32,512]{2,1,0:T(8,128)S(1)}) custom-call(f32[1,64,512]{2,1,0:T(8,128)S(1)} %copy-done.2, bf16[1,8,64,512]{3,2,1,0:T(8,128)(2,1)S(1)} %copy-done.1, f32[1,512]{1,0:T(1,128)S(1)} %copy-done.4, bf16[1,2048,512]{2,1,0:T(8,128)(2,1)S(1)} %copy-done, f32[1,32]{1,0:T(1,128)S(1)} %copy-done.5, ...), custom_call_target="tpu_custom_call" | custom-call | tf_op jit(solution)/shard_map/pallas_call | solution.py:316
  70.5 0.7 copy.14
  71.2 0.6 copy.15
Async XLA Ops:
  1.3 1.6 %copy-start = (bf16[1,2048,512]{2,1,0:T(8,128)(2,1)S(1)}, bf16[1,2048,512]{2,1,0:T(8,128)(2,1)}, u32[]{:S(2)}) copy-start(bf16[1,2048,512]{2,1,0:T(8,128)(2,1)} %moff.1) | copy-start | bytes 6291460
  2.9 1.0 %copy-start.1 = (bf16[1,8,64,512]{3,2,1,0:T(8,128)(2,1)S(1)}, bf16[1,8,64,512]{3,2,1,0:T(8,128)(2,1)}, u32[]{:S(2)}) copy-start(bf16[1,8,64,512]{3,2,1,0:T(8,128)(2,1)} %src.1) | copy-start | bytes 1572868
  3.9 0.9 %copy-start.2 = (f32[1,64,512]{2,1,0:T(8,128)S(1)}, f32[1,64,512]{2,1,0:T(8,128)}, u32[]{:S(2)}) copy-start(f32[1,64,512]{2,1,0:T(8,128)} %x0.1) | copy-start | bytes 393220
  4.8 0.8 %copy-start.3 = (bf16[1,32,512]{2,1,0:T(8,128)(2,1)S(1)}, bf16[1,32,512]{2,1,0:T(8,128)(2,1)}, u32[]{:S(2)}) copy-start(bf16[1,32,512]{2,1,0:T(8,128)(2,1)} %w0.1) | copy-start | bytes 98308
  5.6 0.7 copy-start.4
  6.3 0.7 copy-start.5
  6.9 0.7 copy-start.6
  7.6 0.7 copy-start.7

commit v2 on v1

--- a/solution.py
+++ b/solution.py
@@ -27,13 +27,13 @@
 
 def kernel(
     ns, nb,
-    x0, src, dia, moff, cpl, w0, bkt, par, pos,
+    x0_in, src_in, dia_in, moff, cpl_in, w0_in, bkt_in, par_in, pos_in,
     last, wav,
-    mats, buf, oper, z, hs, p_hi, p_lo, t_hi, t_lo, zp, inc8, rb, samp, wall, iall, call, lhs,
-    m_sem, x_send, x_recv, w_send, w_recv, i_send, i_recv,
+    src, dia, cpl, par, bkt, pos, mats, buf, oper, z, hs, p_hi, p_lo, t_hi, t_lo, zp, inc8, rb, samp, wall, iall, call, lhs,
+    a_sem, m_sem, x_send, x_recv, w_send, w_recv, i_send, i_recv,
 ):
     me_s, me = lax.axis_index("sub"), lax.axis_index("blk")
-    steps, rows, width = src.shape[1:]
+    steps, rows, width = src.shape
     ports = cpl.shape[1]
     stride = width // ports
     all_ports = ports * nb
@@ -42,6 +42,23 @@
     across = lax.rem(me + 2, nb)
     roles = (me, near, across, nb - 1 - me)
 
+    args = [
+        pltpu.make_async_copy(there, here, a_sem.at[r])
+        for r, (there, here) in enumerate(
+            (
+                (bkt_in, bkt),
+                (x0_in.at[0], z),
+                (src_in.at[0], src),
+                (cpl_in, cpl),
+                (w0_in.at[0], wall.at[0, me_s]),
+                (dia_in, dia),
+                (par_in, par),
+                (pos_in, pos),
+            )
+        )
+    ]
+    for load in args:
+        load.start()
     loads = [
         pltpu.make_async_copy(
             moff.at[0, pl.ds(pl.multiple_of(b * width, width), width)], mats.at[r], m_sem.at[r]
@@ -62,6 +79,8 @@
     for peer in roles[1:]:
         pl.semaphore_signal(barrier, inc=1, device_id={"blk": peer}, device_id_type=MESH)
 
+    for load in args:
+        load.wait()
     bucket = bkt[0]
     count = jnp.where(bucket == 0, steps // 4, jnp.where(bucket == 1, steps // 2, steps))
     spacing = jnp.where(bucket == 0, 4, jnp.where(bucket == 1, 2, 1))
@@ -90,9 +109,10 @@
         exchange(g, k, 2).start()
         exchange(g, k, 1).start()
 
-    def finish(g, k):
+    def finish(g, k, meanwhile):
         exchange(g, k, 2).wait_recv()
         exchange(g, k, 3).start()
+        meanwhile()
         total = diagonal * oper[g] + mm(buf[g, k, 0], mats[0])
         exchange(g, k, 1).wait_recv()
         total += mm(buf[g, k, 1], mats[1])
@@ -169,7 +189,7 @@
         def pick(q, chosen):
             return jnp.where(located == q.astype(F32), wall[t, q].astype(F32), chosen)
 
-        chosen = lax.fori_loop(0, ns, pick, jnp.zeros(w0.shape[1:], F32))
+        chosen = lax.fori_loop(0, ns, pick, jnp.zeros(wall.shape[2:], F32))
         iall[t, me] = chosen.astype(BF16)
 
     def inputs(t):
@@ -192,10 +212,8 @@
         == stride * lax.broadcasted_iota(jnp.int32, (ports, width), 0)
     ).astype(F32).astype(BF16)
 
-    z[...] = x0[0]
-    wall[0, me_s] = w0[0]
     call[me] = jnp.broadcast_to(column(cpl[...]), call.shape[1:])
-    first = x0[0] + spacing_f * src[0, fine(0)].astype(F32)
+    first = z[...] + spacing_f * src[fine(0)].astype(F32)
     oper[0] = first
 
     pl.semaphore_wait(barrier, ns - 1 + nb - 1)
@@ -207,7 +225,8 @@
     for load in loads:
         load.wait()
 
-    def keep(h, k, value):
+    def keep(h, k):
+        value = oper[1 + h]
         scale = call[...].reshape(all_ports, call.shape[2])[h * rows : (h + 1) * rows, :1]
         hi, lo = split(scale * value)
         hs[k, h * rows : (h + 1) * rows, :] = hi
@@ -222,36 +241,45 @@
             total += mm((lane + b * width == node).astype(F32).astype(BF16), mats[r])
         oper[1 + h] = total
         post(1 + h, 1, total)
+    def sample(k):
+        hi, lo = split(z[...])
+        zp[k] = mm_nt(pick_ports, hi) + mm_nt(pick_ports, lo)
+
+    def keep_last(k):
+        @pl.when(k >= 0)
+        def _():
+            keep(halves - 1, k)
+
     wait_share(call, 2)
-    for h in range(halves):
-        keep(h, 0, oper[1 + h])
+    for h in range(halves - 1):
+        keep(h, 0)
 
     @pl.loop(0, steps)
     def _(i):
-        total = jnp.where(i < count, finish(0, i), z[...])
+        total = jnp.where(i < count, finish(0, i, lambda: keep_last(i - 1)), z[...])
         z[...] = total
 
         @pl.when(i < steps - 1)
         def _():
-            operand = total + spacing_f * src[0, fine(i + 1)].astype(F32)
+            operand = total + spacing_f * src[fine(i + 1)].astype(F32)
             oper[0] = operand
             post(0, i + 1, operand)
 
-        hi, lo = split(total)
-        zp[i] = mm_nt(pick_ports, hi) + mm_nt(pick_ports, lo)
+        @pl.when(i == 0)
+        def _():
+            sample(0)
 
         @pl.when(i >= 1)
         def _():
             for h in range(halves):
-                value = finish(1 + h, i)
+                work = functools.partial(keep, h - 1, i) if h else functools.partial(sample, i)
+                value = finish(1 + h, i, work)
                 oper[1 + h] = value
 
                 @pl.when(i < steps - 1)
                 def _():
                     post(1 + h, i + 1, value)
 
-                keep(h, i, value)
-
         @pl.when(i == steps // 2 - 1)
         def _():
             wait_waves(0)
@@ -263,6 +291,7 @@
             wait_share(iall.at[0], 0)
             inputs(0)
 
+    keep(halves - 1, steps - 1)
     for k in range(steps):
         for j in range(k + 1):
             there = (
@@ -311,7 +340,6 @@
     all_ports = ports * nb
     groups = 1 + all_ports // rows
     vmem = pl.BlockSpec(memory_space=pltpu.VMEM)
-    smem = pl.BlockSpec(memory_space=pltpu.SMEM)
     dma = pltpu.SemaphoreType.DMA
     return pl.pallas_call(
         functools.partial(kernel, ns, nb),
@@ -319,9 +347,15 @@
             jax.ShapeDtypeStruct(initial_state.shape, F32),
             jax.ShapeDtypeStruct(initial_waves.shape, F32),
         ),
-        in_specs=[vmem, vmem, vmem, pl.BlockSpec(memory_space=pl.ANY), vmem, vmem, smem, vmem, smem],
+        in_specs=[pl.BlockSpec(memory_space=pl.ANY)] * 9,
         out_specs=(vmem, vmem),
         scratch_shapes=[
+            pltpu.VMEM(source.shape[1:], BF16),
+            pltpu.VMEM(inverse_diag.shape, F32),
+            pltpu.VMEM(coupling.shape, F32),
+            pltpu.VMEM(partner.shape, jnp.int32),
+            pltpu.SMEM(bucket.shape, jnp.int32),
+            pltpu.SMEM(position_of.shape, jnp.int32),
             pltpu.VMEM((nb, width, width), BF16),
             pltpu.VMEM((groups, steps, nb, rows, width), BF16),
             pltpu.VMEM((groups, rows, width), F32),
@@ -339,6 +373,7 @@
             pltpu.VMEM((2, nb) + initial_waves.shape[1:], BF16),
             pltpu.VMEM((nb, ports, 128), F32),
             pltpu.VMEM((rows, steps * all_ports), BF16),
+            dma((8,)),
             dma((nb,)),
             dma((groups, 2, 3)),
             dma((groups, 2, 3)),

time: 72.1 us -> 71 us (0.985)
  Pallas kernels: 62.3 us -> 61.2 us
    pallas_call x1, Pallas kernels: 62.3 us -> 61.2 us  [shards(): pl.pallas_call(functools.partial(kernel, ns, nb), out_shape=(jax.ShapeDty...]
where the time goes in v2:
time: 71 us; the launch traced here: 70.7 us
  Pallas kernels  61.2 us (86%)
  local copies, waits for them, and re-layouts  8.22 us (12%)
  between operations  1.3 us (2%)
    pallas_call x1, Pallas kernels, shards(): pl.pallas_call(functools.partial(kernel, ns, nb), out_shape=(jax.ShapeDty...  61.2 us
    unnamed x18, local copies, waits for them, and re-layouts  8.22 us

profile of v2, /device:TPU:0, one launch (start us, length us, event | category | flops | bytes accessed | tf_op | source)
XLA Modules:
  0.0 70.7 jit_solution(2498380057589047371)
XLA Ops:
  1.3 0.0 copy-start
  1.3 1.6 %copy-done = bf16[1,2048,512]{2,1,0:T(8,128)(2,1)S(1)} copy-done((bf16[1,2048,512]{2,1,0:T(8,128)(2,1)S(1)}, bf16[1,2048,512]{2,1,0:T(8,128)(2,1)}, u32[]{:S(2)}) %copy-start) | copy-done | bytes 2097176
  2.9 0.0 copy-start.1
  2.9 1.0 %copy-done.1 = bf16[1,8,64,512]{3,2,1,0:T(8,128)(2,1)S(1)} copy-done((bf16[1,8,64,512]{3,2,1,0:T(8,128)(2,1)S(1)}, bf16[1,8,64,512]{3,2,1,0:T(8,128)(2,1)}, u32[]{:S(2)}) %copy-start.1) | copy-done | bytes 524312
  3.9 0.0 copy-start.2
  3.9 0.9 %copy-done.2 = f32[1,64,512]{2,1,0:T(8,128)S(1)} copy-done((f32[1,64,512]{2,1,0:T(8,128)S(1)}, f32[1,64,512]{2,1,0:T(8,128)}, u32[]{:S(2)}) %copy-start.2) | copy-done | bytes 131096
  4.8 0.0 copy-start.3
  4.8 0.8 %copy-done.3 = bf16[1,32,512]{2,1,0:T(8,128)(2,1)S(1)} copy-done((bf16[1,32,512]{2,1,0:T(8,128)(2,1)S(1)}, bf16[1,32,512]{2,1,0:T(8,128)(2,1)}, u32[]{:S(2)}) %copy-start.3) | copy-done | bytes 32792
  5.6 0.0 copy-start.4
  5.6 0.7 copy-done.4
  6.3 0.0 copy-start.5
  6.3 0.7 copy-done.5
  6.9 0.0 copy-start.6
  6.9 0.7 copy-done.6
  7.6 0.0 copy-start.7
  7.6 0.7 copy-done.7
  8.2 61.2 %shard_map.104 = (f32[1,64,512]{2,1,0:T(8,128)S(1)}, f32[1,32,512]{2,1,0:T(8,128)S(1)}) custom-call(f32[1,64,512]{2,1,0:T(8,128)S(1)} %copy-done.2, bf16[1,8,64,512]{3,2,1,0:T(8,128)(2,1)S(1)} %copy-done.1, f32[1,512]{1,0:T(1,128)S(1)} %copy-done.4, bf16[1,2048,512]{2,1,0:T(8,128)(2,1)S(1)} %copy-done, f32[1,32]{1,0:T(1,128)S(1)} %copy-done.5, ...), custom_call_target="tpu_custom_call" | custom-call | tf_op jit(solution)/shard_map/pallas_call | solution.py:344
  69.4 0.7 copy.14
  70.1 0.6 copy.15
Async XLA Ops:
  1.3 1.6 %copy-start = (bf16[1,2048,512]{2,1,0:T(8,128)(2,1)S(1)}, bf16[1,2048,512]{2,1,0:T(8,128)(2,1)}, u32[]{:S(2)}) copy-start(bf16[1,2048,512]{2,1,0:T(8,128)(2,1)} %moff.1) | copy-start | bytes 6291460
  2.9 1.0 %copy-start.1 = (bf16[1,8,64,512]{3,2,1,0:T(8,128)(2,1)S(1)}, bf16[1,8,64,512]{3,2,1,0:T(8,128)(2,1)}, u32[]{:S(2)}) copy-start(bf16[1,8,64,512]{3,2,1,0:T(8,128)(2,1)} %src_in.1) | copy-start | bytes 1572868
  3.9 0.9 %copy-start.2 = (f32[1,64,512]{2,1,0:T(8,128)S(1)}, f32[1,64,512]{2,1,0:T(8,128)}, u32[]{:S(2)}) copy-start(f32[1,64,512]{2,1,0:T(8,128)} %x0_in.1) | copy-start | bytes 393220
  4.8 0.8 %copy-start.3 = (bf16[1,32,512]{2,1,0:T(8,128)(2,1)S(1)}, bf16[1,32,512]{2,1,0:T(8,128)(2,1)}, u32[]{:S(2)}) copy-start(bf16[1,32,512]{2,1,0:T(8,128)(2,1)} %w0_in.1) | copy-start | bytes 98308
  5.6 0.7 copy-start.4
  6.3 0.7 copy-start.5
  6.9 0.7 copy-start.6
  7.6 0.7 copy-start.7

commit v3 on v2

--- a/solution.py
+++ b/solution.py
@@ -347,7 +347,7 @@
             jax.ShapeDtypeStruct(initial_state.shape, F32),
             jax.ShapeDtypeStruct(initial_waves.shape, F32),
         ),
-        in_specs=[pl.BlockSpec(memory_space=pl.ANY)] * 9,
+        in_specs=[pl.BlockSpec(memory_space=pltpu.HBM)] * 9,
         out_specs=(vmem, vmem),
         scratch_shapes=[
             pltpu.VMEM(source.shape[1:], BF16),

time: 71 us -> 71 us (level)
  no operation moved by 1% of the time
where the time goes in v3:
time: 71 us; the launch traced here: 70.7 us
  Pallas kernels  61.2 us (86%)
  local copies, waits for them, and re-layouts  8.22 us (12%)
  between operations  1.3 us (2%)
    pallas_call x1, Pallas kernels, shards(): pl.pallas_call(functools.partial(kernel, ns, nb), out_shape=(jax.ShapeDty...  61.2 us
    unnamed x18, local copies, waits for them, and re-layouts  8.22 us

profile of v3, /device:TPU:0, one launch (start us, length us, event | category | flops | bytes accessed | tf_op | source)
XLA Modules:
  0.0 70.7 jit_solution(2498380057589047371)
XLA Ops:
  1.3 0.0 copy-start
  1.3 1.6 %copy-done = bf16[1,2048,512]{2,1,0:T(8,128)(2,1)S(1)} copy-done((bf16[1,2048,512]{2,1,0:T(8,128)(2,1)S(1)}, bf16[1,2048,512]{2,1,0:T(8,128)(2,1)}, u32[]{:S(2)}) %copy-start) | copy-done | bytes 2097176
  2.9 0.0 copy-start.1
  2.9 1.0 %copy-done.1 = bf16[1,8,64,512]{3,2,1,0:T(8,128)(2,1)S(1)} copy-done((bf16[1,8,64,512]{3,2,1,0:T(8,128)(2,1)S(1)}, bf16[1,8,64,512]{3,2,1,0:T(8,128)(2,1)}, u32[]{:S(2)}) %copy-start.1) | copy-done | bytes 524312
  3.9 0.0 copy-start.2
  3.9 0.9 %copy-done.2 = f32[1,64,512]{2,1,0:T(8,128)S(1)} copy-done((f32[1,64,512]{2,1,0:T(8,128)S(1)}, f32[1,64,512]{2,1,0:T(8,128)}, u32[]{:S(2)}) %copy-start.2) | copy-done | bytes 131096
  4.8 0.0 copy-start.3
  4.8 0.8 %copy-done.3 = bf16[1,32,512]{2,1,0:T(8,128)(2,1)S(1)} copy-done((bf16[1,32,512]{2,1,0:T(8,128)(2,1)S(1)}, bf16[1,32,512]{2,1,0:T(8,128)(2,1)}, u32[]{:S(2)}) %copy-start.3) | copy-done | bytes 32792
  5.6 0.0 copy-start.4
  5.6 0.7 copy-done.4
  6.3 0.0 copy-start.5
  6.3 0.7 copy-done.5
  6.9 0.0 copy-start.6
  6.9 0.7 copy-done.6
  7.6 0.0 copy-start.7
  7.6 0.7 copy-done.7
  8.2 61.2 %shard_map.104 = (f32[1,64,512]{2,1,0:T(8,128)S(1)}, f32[1,32,512]{2,1,0:T(8,128)S(1)}) custom-call(f32[1,64,512]{2,1,0:T(8,128)S(1)} %copy-done.2, bf16[1,8,64,512]{3,2,1,0:T(8,128)(2,1)S(1)} %copy-done.1, f32[1,512]{1,0:T(1,128)S(1)} %copy-done.4, bf16[1,2048,512]{2,1,0:T(8,128)(2,1)S(1)} %copy-done, f32[1,32]{1,0:T(1,128)S(1)} %copy-done.5, ...), custom_call_target="tpu_custom_call" | custom-call | tf_op jit(solution)/shard_map/pallas_call | solution.py:344
  69.4 0.7 copy.14
  70.1 0.6 copy.15
Async XLA Ops:
  1.3 1.6 %copy-start = (bf16[1,2048,512]{2,1,0:T(8,128)(2,1)S(1)}, bf16[1,2048,512]{2,1,0:T(8,128)(2,1)}, u32[]{:S(2)}) copy-start(bf16[1,2048,512]{2,1,0:T(8,128)(2,1)} %moff.1) | copy-start | bytes 6291460
  2.9 1.0 %copy-start.1 = (bf16[1,8,64,512]{3,2,1,0:T(8,128)(2,1)S(1)}, bf16[1,8,64,512]{3,2,1,0:T(8,128)(2,1)}, u32[]{:S(2)}) copy-start(bf16[1,8,64,512]{3,2,1,0:T(8,128)(2,1)} %src_in.1) | copy-start | bytes 1572868
  3.9 0.9 %copy-start.2 = (f32[1,64,512]{2,1,0:T(8,128)S(1)}, f32[1,64,512]{2,1,0:T(8,128)}, u32[]{:S(2)}) copy-start(f32[1,64,512]{2,1,0:T(8,128)} %x0_in.1) | copy-start | bytes 393220
  4.8 0.8 %copy-start.3 = (bf16[1,32,512]{2,1,0:T(8,128)(2,1)S(1)}, bf16[1,32,512]{2,1,0:T(8,128)(2,1)}, u32[]{:S(2)}) copy-start(bf16[1,32,512]{2,1,0:T(8,128)(2,1)} %w0_in.1) | copy-start | bytes 98308
  5.6 0.7 copy-start.4
  6.3 0.7 copy-start.5
  6.9 0.7 copy-start.6
  7.6 0.7 copy-start.7

commit v4 on v3

--- a/solution.py
+++ b/solution.py
@@ -383,7 +383,7 @@
             dma((3, nb)),
         ],
         compiler_params=pltpu.CompilerParams(
-            collective_id=0, has_side_effects=True, vmem_limit_bytes=48 * 1024 * 1024
+            collective_id=0, has_side_effects=True, vmem_limit_bytes=67043328
         ),
     )(initial_state, source, inverse_diag, inverse_off, coupling, initial_waves, bucket, partner,
       position_of)

time: 71 us -> 66 us (0.930)
  local copies, waits for them, and re-layouts: 8.22 us -> 3.04 us
    unnamed x18 -> x2, local copies, waits for them, and re-layouts: 8.22 us -> 3.04 us
where the time goes in v4:
time: 66 us; the launch traced here: 65.8 us
  Pallas kernels  61.5 us (93%)
  local copies, waits for them, and re-layouts  3.04 us (5%)
  between operations  1.29 us (2%)
    pallas_call x1, Pallas kernels, shards(): pl.pallas_call(functools.partial(kernel, ns, nb), out_shape=(jax.ShapeDty...  61.5 us
    unnamed x2, local copies, waits for them, and re-layouts  3.04 us

profile of v4, /device:TPU:0, one launch (start us, length us, event | category | flops | bytes accessed | tf_op | source)
XLA Modules:
  0.0 65.8 jit_solution(3426447570520825182)
XLA Ops:
  1.3 61.5 %shard_map.104 = (f32[1,64,512]{2,1,0:T(8,128)}, f32[1,32,512]{2,1,0:T(8,128)}) custom-call(f32[1,64,512]{2,1,0:T(8,128)} %x0_in.1, bf16[1,8,64,512]{3,2,1,0:T(8,128)(2,1)} %src_in.1, f32[1,512]{1,0:T(1,128)} %dia_in.1, bf16[1,2048,512]{2,1,0:T(8,128)(2,1)} %moff.1, f32[1,32]{1,0:T(1,128)} %cpl_in.1, bf16[1,32,512]{2,1,0:T(8,128)(2,1)} %w0_in.1, ...), custom_call_target="tpu_custom_call" | custom-call | tf_op jit(solution)/shard_map/pallas_call | solution.py:344
  62.8 1.6 %copy.14 = f32[1,64,512]{2,1,0:T(8,128)} copy(f32[1,64,512]{2,1,0:T(8,128)} %get-tuple-element.4) | data formatting | bytes 262144
  64.4 1.5 %copy.15 = f32[1,32,512]{2,1,0:T(8,128)} copy(f32[1,32,512]{2,1,0:T(8,128)} %get-tuple-element.5) | data formatting | bytes 131072

commit v5 on v4

--- a/solution.py
+++ b/solution.py
@@ -123,51 +123,53 @@
             exchange(g, k, role).wait_send()
         return total
 
-    def wave_copy(t, d):
+    cut = (steps - 2) * rows
+    lanes = (slice(0, steps * rows), slice(0, cut), slice(cut, steps * rows))
+
+    def wave_part(t, owner):
+        return wall.at[min(t, 1), owner, :, lanes[t]]
+
+    def block_part(t, owner):
+        return call.at[owner] if t == 3 else iall.at[min(t, 1), owner, :, lanes[t]]
+
+    def wave_copy(t, d, owner, peer):
         return pltpu.make_async_remote_copy(
-            src_ref=wall.at[t, me_s],
-            dst_ref=wall.at[t, me_s],
+            src_ref=wave_part(t, owner),
+            dst_ref=wave_part(t, owner),
             send_sem=w_send.at[t, d],
-            recv_sem=w_recv.at[t, me_s],
-            device_id={"sub": lax.rem(me_s + d, ns)},
+            recv_sem=w_recv.at[t, owner],
+            device_id={"sub": peer},
             device_id_type=MESH,
         )
 
     def send_waves(t):
         @pl.loop(1, ns)
         def _(d):
-            wave_copy(t, d).start()
+            wave_copy(t, d, me_s, lax.rem(me_s + d, ns)).start()
 
     def wait_waves(t):
         @pl.loop(1, ns)
         def _(d):
             origin = lax.rem(me_s + d, ns)
-            pltpu.make_async_remote_copy(
-                src_ref=wall.at[t, origin],
-                dst_ref=wall.at[t, origin],
-                send_sem=w_send.at[t, d],
-                recv_sem=w_recv.at[t, origin],
-                device_id={"sub": origin},
-                device_id_type=MESH,
-            ).wait_recv()
-
-    def block_copy(ref, t, r, owner):
+            wave_copy(t, d, origin, origin).wait_recv()
+
+    def block_copy(t, r, owner):
         return pltpu.make_async_remote_copy(
-            src_ref=ref.at[owner],
-            dst_ref=ref.at[owner],
+            src_ref=block_part(t, owner),
+            dst_ref=block_part(t, owner),
             send_sem=i_send.at[t, r],
             recv_sem=i_recv.at[t, owner],
             device_id={"blk": roles[r]},
             device_id_type=MESH,
         )
 
-    def share(ref, t):
+    def share(t):
         for r in (2, 3, 1):
-            block_copy(ref, t, r, me).start()
-
-    def wait_share(ref, t):
+            block_copy(t, r, me).start()
+
+    def wait_share(t):
         for r in (1, 2, 3):
-            block_copy(ref, t, r, roles[r]).wait_recv()
+            block_copy(t, r, roles[r]).wait_recv()
 
     square = (
         lax.broadcasted_iota(jnp.int32, (ports, ports), 0)
@@ -187,10 +189,10 @@
         located = lax.fori_loop(0, ns, place, jnp.zeros((ports, 1), F32))
 
         def pick(q, chosen):
-            return jnp.where(located == q.astype(F32), wall[t, q].astype(F32), chosen)
-
-        chosen = lax.fori_loop(0, ns, pick, jnp.zeros(wall.shape[2:], F32))
-        iall[t, me] = chosen.astype(BF16)
+            return jnp.where(located == q.astype(F32), wall[min(t, 1), q, :, lanes[t]].astype(F32), chosen)
+
+        chosen = lax.fori_loop(0, ns, pick, jnp.zeros((ports, lanes[t].stop - lanes[t].start), F32))
+        iall[min(t, 1), me, :, lanes[t]] = chosen.astype(BF16)
 
     def inputs(t):
         for b in range(nb):
@@ -201,10 +203,25 @@
             factor = jnp.where(j < count, spacing_f, 0.0)
             rb[j] = (inc8[fine(j)].astype(F32) * factor).astype(BF16)
 
-    def respond():
-        drive = rb[...].reshape(steps * all_ports, rows)
-        value = mm(t_hi[...], drive) + mm(t_lo[...], drive)
-        samp[...] = zp[...] + value.reshape(steps, ports, rows)
+    def toeplitz(low, high):
+        for k in range(low, high):
+            for j in range(k + 1):
+                there = (
+                    slice(k * ports, (k + 1) * ports),
+                    slice(j * all_ports, (j + 1) * all_ports),
+                )
+                t_hi[there] = p_hi[k - j]
+                t_lo[there] = p_lo[k - j]
+
+    def respond(low, high):
+        drive = rb[:high].reshape(high * all_ports, rows)
+        there = (slice(low * ports, high * ports), slice(0, high * all_ports))
+        value = mm(t_hi[there], drive) + mm(t_lo[there], drive)
+        samp[low:high] = zp[low:high] + value.reshape(high - low, ports, rows)
+
+    def waves_out(low, high):
+        for g in range(low, high):
+            wall[1, me_s, :, g * rows : (g + 1) * rows] = samp[held(g)].astype(BF16)
 
     diagonal = dia[...]
     pick_ports = (
@@ -218,7 +235,7 @@
 
     pl.semaphore_wait(barrier, ns - 1 + nb - 1)
     post(0, 0, first)
-    share(call, 2)
+    share(3)
     send_waves(0)
     t_hi[...] = jnp.zeros_like(t_hi)
     t_lo[...] = jnp.zeros_like(t_lo)
@@ -250,7 +267,7 @@
         def _():
             keep(halves - 1, k)
 
-    wait_share(call, 2)
+    wait_share(3)
     for h in range(halves - 1):
         keep(h, 0)
 
@@ -284,32 +301,35 @@
         def _():
             wait_waves(0)
             select(0)
-            share(iall.at[0], 0)
+            share(0)
 
         @pl.when(i == steps // 2 + 1)
         def _():
-            wait_share(iall.at[0], 0)
+            wait_share(0)
             inputs(0)
 
+        @pl.when(i == steps - 2)
+        def _():
+            toeplitz(0, steps - 2)
+            respond(0, steps - 2)
+            waves_out(0, steps - 2)
+            send_waves(1)
+
     keep(halves - 1, steps - 1)
-    for k in range(steps):
-        for j in range(k + 1):
-            there = (
-                slice(k * ports, (k + 1) * ports),
-                slice(j * all_ports, (j + 1) * all_ports),
-            )
-            t_hi[there] = p_hi[k - j]
-            t_lo[there] = p_lo[k - j]
-    respond()
-    for g in range(steps):
-        wall[1, me_s, :, g * rows : (g + 1) * rows] = samp[held(g)].astype(BF16)
-    send_waves(1)
+    toeplitz(steps - 2, steps)
+    respond(steps - 2, steps)
+    waves_out(steps - 2, steps)
+    send_waves(2)
     wait_waves(1)
     select(1)
-    share(iall.at[1], 1)
-    wait_share(iall.at[1], 1)
+    share(1)
+    wait_waves(2)
+    select(2)
+    share(2)
+    wait_share(1)
+    wait_share(2)
     inputs(1)
-    respond()
+    respond(0, steps)
     for g in range(steps):
         wav[0, :, g * rows : (g + 1) * rows] = samp[held(g)]
     unit = (
@@ -321,16 +341,15 @@
         lhs[:, (m - 1) * all_ports : m * all_ports] = jnp.where(m <= count, turned, 0.0).astype(BF16)
     last[0] = z[...] + mm(lhs[...], hs[...].reshape(steps * all_ports, width))
 
-    for t in range(2):
+    for t in range(3):
 
         @pl.loop(1, ns)
         def _(d):
-            wave_copy(t, d).wait_send()
-
+            wave_copy(t, d, me_s, lax.rem(me_s + d, ns)).wait_send()
+
+    for t in range(4):
         for r in (1, 2, 3):
-            block_copy(iall.at[t], t, r, me).wait_send()
-    for r in (1, 2, 3):
-        block_copy(call, 2, r, me).wait_send()
+            block_copy(t, r, me).wait_send()
 
 
 def shards(ns, nb, initial_state, source, inverse_diag, inverse_off, coupling, initial_waves,
@@ -377,10 +396,10 @@
             dma((nb,)),
             dma((groups, 2, 3)),
             dma((groups, 2, 3)),
-            dma((2, ns)),
-            dma((2, ns)),
-            dma((3, nb)),
-            dma((3, nb)),
+            dma((3, ns)),
+            dma((3, ns)),
+            dma((4, nb)),
+            dma((4, nb)),
         ],
         compiler_params=pltpu.CompilerParams(
             collective_id=0, has_side_effects=True, vmem_limit_bytes=67043328

time: 66 us -> 63.8 us (0.967)
  Pallas kernels: 61.5 us -> 59.3 us
    pallas_call x1, Pallas kernels: 61.5 us -> 59.3 us  [shards(): pl.pallas_call(functools.partial(kernel, ns, nb), out_shape=(jax.ShapeDty...]
where the time goes in v5:
time: 63.8 us; the launch traced here: 63.6 us
  Pallas kernels  59.3 us (93%)
  local copies, waits for them, and re-layouts  3.04 us (5%)
  between operations  1.29 us (2%)
    pallas_call x1, Pallas kernels, shards(): pl.pallas_call(functools.partial(kernel, ns, nb), out_shape=(jax.ShapeDty...  59.3 us
    unnamed x2, local copies, waits for them, and re-layouts  3.04 us

profile of v5, /device:TPU:0, one launch (start us, length us, event | category | flops | bytes accessed | tf_op | source)
XLA Modules:
  0.0 63.6 jit_solution(5682791911299460899)
XLA Ops:
  1.3 59.3 %shard_map.104 = (f32[1,64,512]{2,1,0:T(8,128)}, f32[1,32,512]{2,1,0:T(8,128)}) custom-call(f32[1,64,512]{2,1,0:T(8,128)} %x0_in.1, bf16[1,8,64,512]{3,2,1,0:T(8,128)(2,1)} %src_in.1, f32[1,512]{1,0:T(1,128)} %dia_in.1, bf16[1,2048,512]{2,1,0:T(8,128)(2,1)} %moff.1, f32[1,32]{1,0:T(1,128)} %cpl_in.1, bf16[1,32,512]{2,1,0:T(8,128)(2,1)} %w0_in.1, ...), custom_call_target="tpu_custom_call" | custom-call | tf_op jit(solution)/shard_map/pallas_call | solution.py:363
  60.6 1.6 %copy.14 = f32[1,64,512]{2,1,0:T(8,128)} copy(f32[1,64,512]{2,1,0:T(8,128)} %get-tuple-element.4) | data formatting | bytes 262144
  62.1 1.5 %copy.15 = f32[1,32,512]{2,1,0:T(8,128)} copy(f32[1,32,512]{2,1,0:T(8,128)} %get-tuple-element.5) | data formatting | bytes 131072
